TPU v7x, 32 devices: a whole 2x2x4 slice. The times are simulated.
32 devices in a mesh: row: 8 (over y, x, core), col: 4 (over z).
Axes of the slice: x: 2, y: 2, z: 4, core: 2. Of those that a mesh axis runs over, the one named last changes fastest.
Arguments:
- integrals: float32 [262144, 1024], P(('row', 'col')), may hold values from -0.1875 to 0.1875
- amplitudes: float32 [64, 32768], P(None, ('row', 'col')), may hold values from -6 to 6
Outputs:
- ladder: float32 [16384, 32768], P('row', 'col')
All inputs are finite; a program needn't handle non-finite values.
Results may differ from a plain program's by a relative error of at most 0.00007.
Values sent between devices are 32-bit elements; how exact they have to be, the bound alone decides.
No kernel may reach another device: no remote copies, remote signals or barrier semaphores. Data moves between devices by JAX's collectives and lax.ppermute only.
A program may use at most 448 MiB of HBM per device.

v0:
```python
import jax
import jax.numpy as jnp
from jax import lax
from jax.sharding import PartitionSpec as P

NV = 512
NO = 64
NI = 32
NC = 2


def arrange(flat_amps):
    return flat_amps.reshape(NC, NI, NV, NO).transpose(0, 2, 1, 3).reshape(NC * NV, NI * NO)


def body(integrals, amplitudes):
    flat_amps = lax.all_gather(amplitudes, ("row", "col"), axis=1, tiled=True)
    panel_amps = arrange(flat_amps)
    col_count = lax.axis_size("col")
    local_avals = integrals.shape[0] // NV
    b_width = NV // col_count
    blocks = integrals.reshape(local_avals, col_count, b_width, NC * NV)
    piece = lax.all_to_all(blocks, "col", split_axis=1, concat_axis=0, tiled=True)
    leading = piece.shape[:3]
    result = jnp.dot(
        piece.reshape(-1, NC * NV),
        panel_amps,
        precision=lax.Precision.HIGHEST,
        preferred_element_type=jnp.float32,
    )
    moved = result.reshape(leading + (NI * NO,))
    group_avals = moved.shape[0]
    ladder = moved.reshape(group_avals, b_width, NI, NO).transpose(0, 2, 1, 3)
    return ladder.reshape(group_avals * NI, b_width * NO)


def solution(mesh):
    return jax.shard_map(
        body,
        mesh=mesh,
        in_specs=(P(("row", "col"), None), P(None, ("row", "col"))),
        out_specs=P("row", "col"),
        check_vma=False,
    )
```

profile of v0, /device:TPU:25, one launch (start us, length us, event | category | flops | bytes accessed | tf_op | source)
XLA Modules:
  0.0 1263.3 jit_solution(9209612362592736215)
XLA Ops:
  6.5 23.5 %copy.7 = f32[16,4,128,1024]{3,2,0,1:T(8,128)} copy(f32[16,4,128,1024]{3,2,1,0:T(8,128)} %bitcast.30) | data formatting | bytes 67108864 | tf_op jit(solution)/shard_map/reshape | solution.py:22
  30.1 9.7 all-to-all-start
  39.8 0.0 all-gather.2.cloned.1.call-start
  39.8 0.7 all-gather.2.cloned.1.call-update
  40.5 762.1 %all-gather.2.cloned.1.call-done = f32[64,32768]{1,0:T(8,128)} async-done(((f32[64,1024]{1,0:T(8,128)}), f32[64,32768]{1,0:T(8,128)}) %all-gather.2.cloned.1.call-update) | async-done | bytes 8388624 | tf_op jit(solution)/shard_map/all_gather | solution.py:17
  802.6 13.1 %reshape.18 = f32[2,32,512,64]{3,2,1,0:T(8,128)} reshape(f32[64,32768]{1,0:T(8,128)} %all-gather.2.cloned.1.call-done) | data formatting | bytes 16777216 | tf_op jit(solution)/shard_map/reshape | solution.py:13
  815.7 15.8 %copy.8 = f32[2,512,32,64]{1,0,3,2:T(2,128)} copy(f32[2,512,32,64]{3,1,2,0:T(8,128)} %bitcast.28) | data formatting | bytes 16777216 | tf_op jit(solution)/shard_map/transpose | solution.py:13
  831.5 8.7 copy.11
  840.2 0.0 all-to-all-done
  840.2 221.4 %convolution_bitcast_fusion = f32[64,32,128,64]{2,3,1,0:T(8,128)} fusion(f32[64,128,1024,1]{2,1,3,0:T(8,128)} %bitcast.5, f32[32,64,1024,1]{2,1,0,3:T(8,128)} %bitcast.31), kind=kOutput, calls=%fused_computation | convolution fusion | flops 206158430208 | bytes 109051904 | tf_op jit(solution)/shard_map/dot_general | solution.py:25
  1061.6 87.0 %copy.9 = f32[64,32,128,64]{3,2,1,0:T(8,128)} copy(f32[64,32,128,64]{2,3,1,0:T(8,128)} %convolution_bitcast_fusion) | data formatting | bytes 134217728 | tf_op jit(solution)/shard_map/transpose | solution.py:33
  1148.6 107.9 %reshape.20 = f32[2048,8192]{1,0:T(8,128)} reshape(f32[64,32,128,64]{3,2,1,0:T(8,128)} %copy.9) | data formatting | bytes 134217728 | tf_op jit(solution)/shard_map/reshape | solution.py:34
Async XLA Ops:
  30.1 810.1 %all-to-all-start = ((f32[16,4,128,1024]{3,2,0,1:T(8,128)}), f32[16,4,128,1024]{3,2,0,1:T(8,128)}, u32[]{:S(2)}, u32[]{:S(2)}) async-start(f32[16,4,128,1024]{3,2,0,1:T(8,128)} %copy.7), calls=%async_computation | async-start | bytes 67108864 | tf_op jit(solution)/shard_map/all_to_all | solution.py:23
  39.8 762.8 %all-gather.2.cloned.1.call-start = ((), (), s32[]{:S(2)}) async-start(), calls=%async_computation.1 | async-start | bytes 8650752 | tf_op jit(solution)/shard_map/all_gather | solution.py:17
Sparse Core Ops, SparseCore 0:
  43.6 758.9 all-gather.1
where the time goes:
time: 1270 us; the launch traced here: 1260 us
  waiting for transfers between devices  763 us (60%)
  local copies, waits for them, and re-layouts  256 us (20%)
  matrix products  221 us (17%)
  between operations  13.4 us (1%)
    all_gather x1, waiting for transfers between devices, body(): flat_amps = lax.all_gather(amplitudes, ('row', 'col'), axis=1, tiled=True)  762 us
    dot_general x1, matrix products, body(): jnp.dot(piece.reshape(-1, NC * NV), panel_amps, precision=lax.Precision.H...  221 us
    reshape x1, local copies, waits for them, and re-layouts, body(): return ladder.reshape(group_avals * NI, b_width * NO)  108 us
    transpose x1, local copies, waits for them, and re-layouts, body(): ladder = moved.reshape(group_avals, b_width, NI, NO).transpose(0, 2, 1, 3)  87 us
  transfers between devices with their start and end apart: 2, of which 1 were waited for; matrix products, arithmetic and copies ran while one was open for 3% of the time, Pallas kernels for 0%

commit v1 on v0

--- a/solution.py
+++ b/solution.py
@@ -14,7 +14,14 @@
 
 
 def body(integrals, amplitudes):
-    flat_amps = lax.all_gather(amplitudes, ("row", "col"), axis=1, tiled=True)
+    ways, here = (lax.axis_size(("row", "col")), lax.axis_index(("row", "col")))
+    flat_amps, reach = (amplitudes, 1)
+    while reach < ways:
+        theirs = lax.ppermute(flat_amps, ("row", "col"), [(d, d ^ reach) for d in range(ways)])
+        mine_first = jnp.concatenate([flat_amps, theirs], axis=1)
+        theirs_first = jnp.concatenate([theirs, flat_amps], axis=1)
+        flat_amps = jnp.where(here & reach == 0, mine_first, theirs_first)
+        reach = 2 * reach
     panel_amps = arrange(flat_amps)
     col_count = lax.axis_size("col")
     local_avals = integrals.shape[0] // NV

time: 1270 us -> 1460 us (1.15)
  waiting for transfers between devices: 763 us -> 879 us
  local copies, waits for them, and re-layouts: 256 us -> 301 us
  matrix products: 221 us -> 237 us
  other arithmetic: 0 us -> 15.9 us
    ppermute x0 -> x5, waiting for transfers between devices: none -> 879 us  [body(): lax.ppermute(flat_amps, ('row', 'col'), [(d, d ^ reach) for d in range(wa...]
    all_gather x1 -> x0, waiting for transfers between devices: 762 us -> none  [body(): flat_amps = lax.all_gather(amplitudes, ('row', 'col'), axis=1, tiled=True)]
    another operation x0 -> x1, local copies, waits for them, and re-layouts: none -> 88 us  [body(): ladder = moved.reshape(group_avals, b_width, NI, NO).transpose(0, 2, 1, 3)]
    transpose x1 -> x0, local copies, waits for them, and re-layouts: 87 us -> none  [body(): ladder = moved.reshape(group_avals, b_width, NI, NO).transpose(0, 2, 1, 3)]
    unnamed x1 -> x4, local copies, waits for them, and re-layouts: 8.67 us -> 53 us
    select_n x0 -> x5, other arithmetic: none -> 15.9 us  [body(): flat_amps = jnp.where(here & reach == 0, mine_first, theirs_first)]
    dot_general x1, matrix products: 221 us -> 237 us  [body(): jnp.dot(piece.reshape(-1, NC * NV), panel_amps, precision=lax.Precision.H...]
  transfers between devices with their start and end apart: 2 -> 6, of which waited for: 1 -> 5; matrix products, arithmetic and copies ran while one was open for 3% -> 4% of each run, Pallas kernels for 0% -> 0%
where the time goes in v1:
time: 1460 us; the launch traced here: 1450 us
  waiting for transfers between devices  879 us (60%)
  local copies, waits for them, and re-layouts  301 us (21%)
  matrix products  237 us (16%)
  other arithmetic  15.9 us (1%)
  starting transfers between devices  15.1 us (1%)
    ppermute x5, waiting for transfers between devices, body(): lax.ppermute(flat_amps, ('row', 'col'), [(d, d ^ reach) for d in range(wa...  879 us
    dot_general x1, matrix products, body(): jnp.dot(piece.reshape(-1, NC * NV), panel_amps, precision=lax.Precision.H...  237 us
    reshape x1, local copies, waits for them, and re-layouts, body(): return ladder.reshape(group_avals * NI, b_width * NO)  108 us
    another operation x1, local copies, waits for them, and re-layouts, body(): ladder = moved.reshape(group_avals, b_width, NI, NO).transpose(0, 2, 1, 3)  88 us
    unnamed x4, local copies, waits for them, and re-layouts  53 us
  transfers between devices with their start and end apart: 6, of which 5 were waited for; matrix products, arithmetic and copies ran while one was open for 4% of the time, Pallas kernels for 0%

profile of v1, /device:TPU:25, one launch (start us, length us, event | category | flops | bytes accessed | tf_op | source)
XLA Modules:
  0.0 1448.3 jit_solution(17161594041527176394)
XLA Ops:
  0.0 23.5 %copy.10 = f32[16,4,128,1024]{3,2,0,1:T(8,128)} copy(f32[16,4,128,1024]{3,2,1,0:T(8,128)} %bitcast.26) | data formatting | bytes 67108864 | tf_op jit(solution)/shard_map/reshape | solution.py:29
  23.5 0.0 copy-start
  23.5 9.8 all-to-all-start
  33.4 0.0 copy-done
  33.4 0.2 collective-permute-start
  33.6 544.6 %collective-permute-done = f32[64,1024]{1,0:T(8,128)S(1)} collective-permute-done((f32[64,1024]{1,0:T(8,128)S(1)}, f32[64,1024]{1,0:T(8,128)S(1)}, u32[]{:S(2)}, u32[]{:S(2)}) %collective-permute-start) | collective-permute-done | bytes 262176 | tf_op jit(solution)/shard_map/ppermute | solution.py:20
  578.3 0.8 collective-permute-start.1
  579.1 196.4 %collective-permute-done.1 = f32[64,2048]{1,0:T(8,128)S(1)} collective-permute-done((f32[64,2048]{1,0:T(8,128)S(1)}, f32[64,2048]{1,0:T(8,128)S(1)}, u32[]{:S(2)}, u32[]{:S(2)}) %collective-permute-start.1) | collective-permute-done | bytes 524320 | tf_op jit(solution)/shard_map/ppermute | solution.py:20
  775.5 0.1 maximum_select_fusion.3
  775.7 1.3 collective-permute-start.2
  777.0 2.4 collective-permute-done.2
  779.4 1.8 maximum_select_fusion.2
  781.2 1.5 collective-permute-start.3
  782.6 45.5 %collective-permute-done.3 = f32[64,8192]{1,0:T(8,128)} collective-permute-done((f32[64,8192]{1,0:T(8,128)S(1)}, f32[64,8192]{1,0:T(8,128)}, u32[]{:S(2)}, u32[]{:S(2)}) %collective-permute-start.3) | collective-permute-done | bytes 2097184 | tf_op jit(solution)/shard_map/ppermute | solution.py:20
  828.2 4.7 maximum_select_fusion.1
  832.9 1.4 collective-permute-start.4
  834.3 89.8 %collective-permute-done.4 = f32[64,16384]{1,0:T(8,128)} collective-permute-done((f32[64,16384]{1,0:T(8,128)}, f32[64,16384]{1,0:T(8,128)}, u32[]{:S(2)}, u32[]{:S(2)}) %collective-permute-start.4) | collective-permute-done | bytes 4194336 | tf_op jit(solution)/shard_map/ppermute | solution.py:20
  924.1 9.2 maximum_select_fusion
  933.3 13.1 select_n.54
  946.5 15.8 %copy.9 = f32[2,512,32,64]{1,0,3,2:T(2,128)} copy(f32[2,512,32,64]{3,1,2,0:T(8,128)} %bitcast.24) | data formatting | bytes 16777216 | tf_op jit(solution)/shard_map/transpose | solution.py:13
  962.3 8.7 copy.12
  970.9 0.0 all-to-all-done
  970.9 237.1 %convolution_bitcast_fusion = f32[256,8,64,128]{3,1,2,0:T(8,128)} fusion(f32[1024,2048]{0,1:T(8,128)} %bitcast.27, f32[8192,1024]{1,0:T(8,128)} %bitcast.4), kind=kOutput, calls=%fused_computation | convolution fusion | flops 206158430208 | bytes 109051904 | tf_op jit(solution)/shard_map/dot_general | solution.py:32
  1208.1 44.3 %copy.13 = f32[256,8,64,128]{3,2,1,0:T(8,128)} copy(f32[256,8,64,128]{3,1,2,0:T(8,128)} %convolution_bitcast_fusion) | data formatting | bytes 134217728
  1252.3 88.0 %copy.11 = f32[64,128,32,64]{3,1,2,0:T(8,128)} copy(f32[64,128,32,64]{1,0,3,2:T(8,128)} %bitcast.18) | data formatting | bytes 134217728 | tf_op jit(solution)/shard_map/reshape;reshape | solution.py:40
  1340.4 107.9 %reshape.21 = f32[2048,8192]{1,0:T(8,128)} reshape(f32[64,32,128,64]{3,2,1,0:T(8,128)} %bitcast.6) | data formatting | bytes 134217728 | tf_op jit(solution)/shard_map/reshape | solution.py:41
  (1 shorter events, 0.0 us)
Async XLA Ops:
  23.5 9.9 copy-start
  23.5 947.4 %all-to-all-start = ((f32[16,4,128,1024]{3,2,0,1:T(8,128)}), f32[16,4,128,1024]{3,2,0,1:T(8,128)}, u32[]{:S(2)}, u32[]{:S(2)}) async-start(f32[16,4,128,1024]{3,2,0,1:T(8,128)} %copy.10), calls=%async_computation | async-start | bytes 67108864 | tf_op jit(solution)/shard_map/all_to_all | solution.py:30
  33.4 544.8 %collective-permute-start = (f32[64,1024]{1,0:T(8,128)S(1)}, f32[64,1024]{1,0:T(8,128)S(1)}, u32[]{:S(2)}, u32[]{:S(2)}) collective-permute-start(f32[64,1024]{1,0:T(8,128)S(1)} %copy-done), channel_id=1, source_target_pairs={{0,1},{1,0},{2,3},{3,2},{4,5},{5,4},{6,7},{7,6},{8,9},{9,8},{10,11... | collective-permute-start | bytes 786440 | tf_op jit(solution)/shard_map/ppermute | solution.py:20
  578.3 197.3 %collective-permute-start.1 = (f32[64,2048]{1,0:T(8,128)S(1)}, f32[64,2048]{1,0:T(8,128)S(1)}, u32[]{:S(2)}, u32[]{:S(2)}) collective-permute-start(f32[64,2048]{1,0:T(8,128)S(1)} %maximum_select_fusion.4), channel_id=1, source_target_pairs={{0,2},{1,3},{2,0},{3,1},{4,6},{5,7},{6,4},{7,5},{8,10},{9,11},{10,... | collective-permute-start | bytes 1572872 | tf_op jit(solution)/shard_map/ppermute | solution.py:20
  775.7 3.7 collective-permute-start.2
  781.2 47.0 %collective-permute-start.3 = (f32[64,8192]{1,0:T(8,128)S(1)}, f32[64,8192]{1,0:T(8,128)}, u32[]{:S(2)}, u32[]{:S(2)}) collective-permute-start(f32[64,8192]{1,0:T(8,128)S(1)} %maximum_select_fusion.2), channel_id=1, source_target_pairs={{0,8},{1,9},{2,10},{3,11},{4,12},{5,13},{6,14},{7,15},{8,0},{9,1},... | collective-permute-start | bytes 6291464 | tf_op jit(solution)/shard_map/ppermute | solution.py:20
  832.9 91.2 %collective-permute-start.4 = (f32[64,16384]{1,0:T(8,128)}, f32[64,16384]{1,0:T(8,128)}, u32[]{:S(2)}, u32[]{:S(2)}) collective-permute-start(f32[64,16384]{1,0:T(8,128)} %maximum_select_fusion.1), channel_id=1, source_target_pairs={{0,16},{1,17},{2,18},{3,19},{4,20},{5,21},{6,22},{7,23},{8,24},{9,... | collective-permute-start | bytes 12582920 | tf_op jit(solution)/shard_map/ppermute | solution.py:20
